TPU v7x, 512 devices: a whole 4x4x16 slice. The times are simulated.
512 devices in a mesh: gx: 32 (over z, core), gy: 16 (over y, x).
Axes of the slice: x: 4, y: 4, z: 16, core: 2. Of those that a mesh axis runs over, the one named last changes fastest.
Arguments:
- tokens: bfloat16 [8192, 2048], P('gx'), may hold values from -6 to 6
- lengths: int32 [4], replicated, may hold values from 1 to 4096, 8192 in all
- adapter_of_request: int32 [4], replicated, may hold values from 0 to 15
- adapter_storage_slot: int32 [16], replicated, may hold values from 0 to 15, each once
- page_cache_slot: int32 [1024], P('gx'), may hold values from 0 to 1023, as said below
- query_key_value_weight: bfloat16 [2048, 16, 384], P(None, 'gy'), may hold values from -4 to 4
- adapter_down_maps: bfloat16 [16, 2048, 48], P('gy'), may hold values from -0.125 to 0.125
- adapter_up_maps: bfloat16 [16, 3, 16, 16, 128], P(None, None, None, 'gy'), may hold values from -1.5 to 1.5
- query_norm_gain: float32 [16, 128], P('gy'), may hold values from 0.25 to 1.75
- key_norm_gain: float32 [16, 128], P('gy'), may hold values from 0.25 to 1.75
- output_weight: bfloat16 [16, 128, 2048], P('gy'), may hold values from -0.125 to 0.125
- post_norm_gain: float32 [2048], replicated, may hold values from 0.25 to 1.75
Outputs:
- mixed: bfloat16 [8192, 2048], P('gx')
- kv_cache: bfloat16 [1024, 8, 16, 256], P('gx', None, 'gy')
Inputs may be any that keep to these rules, and one draw needn't show every extreme that they name: `page_cache_slot`: each slot appears once; the 32 pages of the tokens of one index of gx have exactly 1 slot among the 32 slots held by each index k of gx (slots k * 32 onward).
All inputs are finite; a program needn't handle non-finite values.
Results may differ from a plain program's by a relative error of at most 0.017.
Values may be sent and summed in bfloat16 or wider, within the bound.
No kernel may reach another device: no remote copies, remote signals or barrier semaphores. Data moves between devices by JAX's collectives and lax.ppermute only.
A program may use at most 64 MiB of HBM per device.

v0:
```python
import jax
import jax.numpy as jnp
from jax import lax
from jax.sharding import PartitionSpec as P

MODEL_WIDTH = 2048
HEAD_SIZE = 128
ADAPTER_RANK = 16
PAGE = 8


def request_of(rows, ends):
    return jnp.sum((ends[None, :] <= rows[:, None]).astype(jnp.int32), axis=1)


def lookup(index, table):
    match = index[:, None] == jnp.arange(table.shape[0])[None, :]
    return jnp.sum(jnp.where(match, table[None, :], 0), axis=1)


def rotate(values, positions):
    half = values.shape[-1] // 2
    freq = 500000.0 ** (-(jnp.arange(half).astype(jnp.float32) * 2.0) / values.shape[-1])
    angle = positions.astype(jnp.float32)[:, None] * freq[None, :]
    cosine = jnp.cos(angle)[:, None, :]
    sine = jnp.sin(angle)[:, None, :]
    first = values[..., :half]
    second = values[..., half:]
    return jnp.concatenate(
        [first * cosine - second * sine, second * cosine + first * sine], axis=-1
    )


def shards(
    tokens,
    lengths,
    adapter_of_request,
    adapter_storage_slot,
    page_cache_slot,
    query_key_value_weight,
    adapter_down_maps,
    adapter_up_maps,
    query_norm_gain,
    key_norm_gain,
    output_weight,
    post_norm_gain,
):
    count = tokens.shape[0]
    group = lax.axis_index("gx")
    member = lax.axis_index("gy")
    rows = group * count + jnp.arange(count)
    ends = jnp.cumsum(lengths)
    starts = ends - lengths
    request = request_of(rows, ends)
    positions = rows - lookup(request, starts)
    slots = lookup(lookup(request, adapter_of_request), adapter_storage_slot)
    resident_count = adapter_down_maps.shape[0]
    held = member * resident_count + jnp.arange(resident_count)
    reduced_rows = jnp.einsum(
        "zm,ump->zup", tokens, adapter_down_maps, preferred_element_type=jnp.float32
    )
    chosen = (slots[:, None] == held[None, :]).astype(jnp.float32)
    partial_low = jnp.sum(chosen[:, :, None] * reduced_rows, axis=1)
    low = lax.psum(partial_low.astype(jnp.bfloat16), "gy")
    adapter_count_total = adapter_up_maps.shape[0]
    selector = (slots[:, None] == jnp.arange(adapter_count_total)[None, :]).astype(jnp.bfloat16)
    expanded_rows = selector[:, :, None, None] * low.reshape(count, 1, 3, ADAPTER_RANK)
    adapter_update = jnp.einsum(
        "dzqi,zqibj->dqbj", expanded_rows, adapter_up_maps, preferred_element_type=jnp.float32
    )
    base = jnp.einsum(
        "td,dhe->the", tokens, query_key_value_weight, preferred_element_type=jnp.float32
    )
    query = base[..., :HEAD_SIZE] + adapter_update[:, 0]
    key_raw = base[..., HEAD_SIZE : 2 * HEAD_SIZE] + adapter_update[:, 1]
    value = base[..., 2 * HEAD_SIZE :] + adapter_update[:, 2]
    query_sq, key_sq = lax.psum(
        (jnp.sum(query * query, axis=(1, 2)), jnp.sum(key_raw * key_raw, axis=(1, 2))), "gy"
    )
    query_n = (
        query * lax.rsqrt(query_sq / MODEL_WIDTH + 1e-06)[:, None, None] * query_norm_gain[None]
    )
    key_n = key_raw * lax.rsqrt(key_sq / MODEL_WIDTH + 1e-06)[:, None, None] * key_norm_gain[None]
    query_b = rotate(query_n, positions).astype(jnp.bfloat16)
    key_b = rotate(key_n, positions).astype(jnp.bfloat16)
    value_b = value.astype(jnp.bfloat16)
    heads_here = query_key_value_weight.shape[1]
    pages_here = count // PAGE
    pages = jnp.concatenate([key_b, value_b], axis=-1).reshape(
        pages_here, PAGE, heads_here, 2 * HEAD_SIZE
    )
    order = jnp.argsort(page_cache_slot)
    got_pages, got_slots = (
        lax.all_to_all(pages[order], "gx", split_axis=0, concat_axis=0, tiled=True),
        lax.all_to_all(page_cache_slot[order], "gx", split_axis=0, concat_axis=0, tiled=True),
    )
    kv_cache = got_pages[jnp.argsort(got_slots)]
    scale = HEAD_SIZE ** (-0.5)

    def attend(carry, key_vectors, values, key_rows):
        best, total, accum = carry
        key_request = request_of(key_rows, ends)
        scores = (
            jnp.einsum("the,khe->htk", query_b, key_vectors, preferred_element_type=jnp.float32)
            * scale
        )
        allowed = (request[:, None] == key_request[None, :]) & (key_rows[None, :] <= rows[:, None])
        masked = jnp.where(allowed[None], scores, -1e30)
        new_best = jnp.maximum(best, jnp.max(masked, axis=-1))
        weights = jnp.where(allowed[None], jnp.exp(scores - new_best[..., None]), 0.0)
        factor = jnp.exp(best - new_best)
        total = total * factor + jnp.sum(weights, axis=-1)
        update = jnp.einsum(
            "htk,khe->hte", weights.astype(jnp.bfloat16), values, preferred_element_type=jnp.float32
        )
        accum = accum * factor[..., None] + update
        return (new_best, total, accum)

    initial = (
        jnp.full((heads_here, count), -1e30, jnp.float32),
        jnp.zeros((heads_here, count), jnp.float32),
        jnp.zeros((heads_here, count, HEAD_SIZE), jnp.float32),
    )
    key_vectors = lax.all_gather(key_b, "gx", axis=0, tiled=True)
    values = lax.all_gather(value_b, "gx", axis=0, tiled=True)
    size = key_vectors.shape[0]
    block = 512

    def one_block(index, state):
        begin = index * block
        key_part = lax.dynamic_slice_in_dim(key_vectors, begin, block, 0)
        value_part = lax.dynamic_slice_in_dim(values, begin, block, 0)
        key_rows = begin + jnp.arange(block)
        return attend(state, key_part, value_part, key_rows)

    best, total, accum = lax.fori_loop(0, size // block, one_block, initial)
    attn = (accum / total[..., None]).astype(jnp.bfloat16)
    partial_out = jnp.einsum("hte,hed->td", attn, output_weight, preferred_element_type=jnp.float32)
    output = lax.psum(partial_out.astype(jnp.bfloat16), "gy").astype(jnp.float32)
    normed = (
        output
        * lax.rsqrt(jnp.mean(output * output, axis=1) + 1e-06)[:, None]
        * post_norm_gain[None, :]
    )
    mixed = (tokens.astype(jnp.float32) + normed).astype(jnp.bfloat16)
    return (mixed, kv_cache)


def solution(mesh):
    return jax.shard_map(
        shards,
        mesh=mesh,
        in_specs=(
            P("gx", None),
            P(),
            P(),
            P(),
            P("gx"),
            P(None, "gy", None),
            P("gy", None, None),
            P(None, None, None, "gy", None),
            P("gy", None),
            P("gy", None),
            P("gy", None, None),
            P(),
        ),
        out_specs=(P("gx", None), P("gx", None, "gy", None)),
        check_vma=False,
    )
```

profile of v0, /device:TPU:32, one launch (start us, length us, event | category | flops | bytes accessed | tf_op | source)
XLA Modules:
  0.0 445.1 jit_solution(11517718805805738873)
XLA Ops:
  10.4 1.7 fusion.33
  12.2 74.6 %psum.28 = bf16[256,3,16]{0,2,1:T(8,128)(2,1)S(1)} all-reduce(bf16[256,3,16]{0,2,1:T(8,128)(2,1)S(1)} %bitcast.114), channel_id=1, replica_groups=mesh['gx'=32,'gy'=16] {'gy'}, use_global_device_ids=true, to_apply=%region_4.5 | all-reduce | flops 12288 | bytes 49152 | tf_op jit(solution)/shard_map/psum | solution.py:64
  86.8 1.9 fusion.30
  89.2 35.5 %all-reduce = (f32[256]{0:T(256)S(1)}, f32[256]{0:T(256)S(1)}) all-reduce(f32[256]{0:T(256)S(1)} %get-tuple-element.231, f32[256]{0:T(256)S(1)} %get-tuple-element.230), channel_id=1, replica_groups=mesh['gx'=32,'gy'=16] {'gy'}, use_global_device_ids=true, to_apply=%region_6.7 | all-reduce | flops 512 | bytes 4096 | tf_op jit(solution)/shard_map/psum | solution.py:77
  127.7 71.4 %all-gather.3.cloned.1.call-done = bf16[8192,1,128]{2,0,1:T(8,128)(2,1)} async-done(((bf16[256,1,128]{2,0,1:T(8,128)(2,1)}), bf16[8192,1,128]{2,0,1:T(8,128)(2,1)}) %all-gather.3.cloned.1.call-update) | async-done | bytes 2097168 | tf_op jit(solution)/shard_map/all_gather | solution.py:124
  199.1 71.5 %all-gather.5.cloned.1.call-done = bf16[8192,1,128]{2,0,1:T(8,128)(2,1)} async-done(((bf16[256,1,128]{2,0,1:T(8,128)(2,1)}), bf16[8192,1,128]{2,0,1:T(8,128)(2,1)}) %all-gather.5.cloned.1.call-update) | async-done | bytes 2097168 | tf_op jit(solution)/shard_map/all_gather | solution.py:125
  270.6 47.3 %while.18 = (s32[]{:T(128)}, f32[1,256]{1,0:T(1,128)S(1)}, f32[1,256]{1,0:T(1,128)S(1)}, f32[1,256,128]{2,1,0:T(8,128)S(1)}, s32[256]{0:T(256)S(1)}, /*index=5*/...) while((s32[]{:T(128)}, f32[1,256]{1,0:T(1,128)S(1)}, ...), condition=%wide.region_14.15_spmd.clone, body=%wide.region_10.14_spmd.clone.sunk | while | flops 69574144 | bytes 2204895 | solution.py:136
  272.2 1.4 fusion.75
  275.2 1.4 fusion.75
  278.1 1.4 fusion.75
  281.1 1.4 fusion.75
  284.0 1.4 fusion.75
  287.0 1.4 fusion.75
  289.9 1.4 fusion.75
  292.9 1.4 fusion.75
  295.8 1.4 fusion.75
  298.8 1.4 fusion.75
  301.8 1.4 fusion.75
  304.7 1.4 fusion.75
  307.7 1.4 fusion.75
  310.6 1.4 fusion.75
  316.5 1.4 fusion.75
  317.9 1.5 convolution_convert_fusion
  319.4 1.7 sort.31
  322.5 8.5 %all-to-all-start.1 = ((s32[32,1,1]{2,1,0:T(1,128)}), s32[32,1,1]{2,1,0:T(1,128)S(1)}, u32[]{:S(2)}, u32[]{:S(2)}) async-start(s32[32,1,1]{2,1,0:T(1,128)} %copy.31), calls=%async_computation.1 | async-start | bytes 32768 | tf_op jit(solution)/shard_map/all_to_all | solution.py:95
  332.4 9.8 %all-to-all-done.1 = s32[32,1,1]{2,1,0:T(1,128)S(1)} async-done(((s32[32,1,1]{2,1,0:T(1,128)}), s32[32,1,1]{2,1,0:T(1,128)S(1)}, u32[]{:S(2)}, u32[]{:S(2)}) %all-to-all-start.1) | async-done | bytes 160 | tf_op jit(solution)/shard_map/all_to_all | solution.py:95
  342.2 5.0 %all-to-all-start = ((bf16[32,8,1,256]{3,1,2,0:T(8,128)(2,1)}), bf16[32,8,1,256]{3,1,2,0:T(8,128)(2,1)S(1)}, u32[]{:S(2)}, u32[]{:S(2)}) async-start(bf16[32,8,1,256]{3,1,2,0:T(8,128)(2,1)} %bitcast.26), calls=%async_computation | async-start | bytes 262144 | tf_op jit(solution)/shard_map/all_to_all | solution.py:94
  347.9 1.7 sort.32
  349.6 13.7 %all-to-all-done = bf16[32,8,1,256]{3,1,2,0:T(8,128)(2,1)S(1)} async-done(((bf16[32,8,1,256]{3,1,2,0:T(8,128)(2,1)}), bf16[32,8,1,256]{3,1,2,0:T(8,128)(2,1)S(1)}, u32[]{:S(2)}, u32[]{:S(2)}) %all-to-all-start) | async-done | bytes 131104 | tf_op jit(solution)/shard_map/all_to_all | solution.py:94
  364.6 69.8 %all-reduce.3.cloned.1.call-done = bf16[256,2048]{1,0:T(8,128)(2,1)} async-done(((bf16[256,2048]{1,0:T(8,128)(2,1)}), bf16[256,2048]{1,0:T(8,128)(2,1)}) %all-reduce.3.cloned.1.call-update) | async-done | bytes 1048592 | tf_op jit(solution)/shard_map/psum | solution.py:139
  434.3 1.5 fusion.24
  435.9 2.6 fusion.27
  (186 shorter events, 37.0 us)
Async XLA Ops:
  7.2 79.6 %copy-start = (bf16[2048,1,384]{2,0,1:T(8,128)(2,1)S(1)}, bf16[2048,1,384]{2,0,1:T(8,128)(2,1)}, u32[]{:S(2)}) copy-start(bf16[2048,1,384]{2,0,1:T(8,128)(2,1)} %param.19) | copy-start | bytes 4718596
  7.2 191.9 %all-gather.3.cloned.1.call-start = ((), (), s32[]{:S(2)}) async-start(), calls=%async_computation.2 | async-start | bytes 2162688 | tf_op jit(solution)/shard_map/all_gather | solution.py:124
  10.4 78.3 %copy-start.8 = (bf16[16,3,16,1,128]{4,2,3,1,0:T(8,128)(2,1)S(1)}, bf16[16,3,16,1,128]{4,2,3,1,0:T(8,128)(2,1)}, u32[]{:S(2)}) copy-start(bf16[16,3,16,1,128]{4,2,3,1,0:T(8,128)(2,1)} %param.21) | copy-start | bytes 589828
  88.7 36.0 %copy-start.6 = (f32[1,128]{1,0:T(1,128)S(1)}, f32[1,128]{1,0:T(1,128)}, u32[]{:S(2)}) copy-start(f32[1,128]{1,0:T(1,128)} %param.23) | copy-start | bytes 1540
  88.7 36.0 %copy-start.7 = (f32[1,128]{1,0:T(1,128)S(1)}, f32[1,128]{1,0:T(1,128)}, u32[]{:S(2)}) copy-start(f32[1,128]{1,0:T(1,128)} %param.22) | copy-start | bytes 1540
  126.8 143.8 %all-gather.5.cloned.1.call-start = ((), (), s32[]{:S(2)}) async-start(), calls=%async_computation.3 | async-start | bytes 2162688 | tf_op jit(solution)/shard_map/all_gather | solution.py:125
  127.5 306.8 %all-reduce.3.cloned.1.call-start = ((), (), s32[]{:S(2)}) async-start(), calls=%async_computation.4 | async-start | bytes 2097152 | tf_op jit(solution)/shard_map/psum | solution.py:139
  270.6 47.3 %copy-start.4 = (bf16[1,128,2048]{2,1,0:T(8,128)(2,1)S(1)}, bf16[1,128,2048]{2,1,0:T(8,128)(2,1)}, u32[]{:S(2)}) copy-start(bf16[1,128,2048]{2,1,0:T(8,128)(2,1)} %param.24) | copy-start | bytes 1572868
  317.9 1.5 copy-start.1
  317.9 13.1 %copy-start.3 = (bf16[256,1,128]{2,0,1:T(8,128)(2,1)S(1)}, bf16[256,1,128]{2,0,1:T(8,128)(2,1)}, u32[]{:S(2)}) copy-start(bf16[256,1,128]{2,0,1:T(8,128)(2,1)} %get-tuple-element.260) | copy-start | bytes 196612
  319.4 116.5 %copy-start.2 = (bf16[256,2048]{1,0:T(8,128)(2,1)S(1)}, bf16[256,2048]{1,0:T(8,128)(2,1)}, u32[]{:S(2)}) copy-start(bf16[256,2048]{1,0:T(8,128)(2,1)} %param.14) | copy-start | bytes 3145732
  319.4 116.5 %copy-start.5 = (f32[2048]{0:T(1024)S(1)}, f32[2048]{0:T(1024)}, u32[]{:S(2)}) copy-start(f32[2048]{0:T(1024)} %param.25) | copy-start | bytes 24580
  322.5 19.7 %all-to-all-start.1 = ((s32[32,1,1]{2,1,0:T(1,128)}), s32[32,1,1]{2,1,0:T(1,128)S(1)}, u32[]{:S(2)}, u32[]{:S(2)}) async-start(s32[32,1,1]{2,1,0:T(1,128)} %copy.31), calls=%async_computation.1 | async-start | bytes 32768 | tf_op jit(solution)/shard_map/all_to_all | solution.py:95
  342.2 21.1 %all-to-all-start = ((bf16[32,8,1,256]{3,1,2,0:T(8,128)(2,1)}), bf16[32,8,1,256]{3,1,2,0:T(8,128)(2,1)S(1)}, u32[]{:S(2)}, u32[]{:S(2)}) async-start(bf16[32,8,1,256]{3,1,2,0:T(8,128)(2,1)} %bitcast.26), calls=%async_computation | async-start | bytes 262144 | tf_op jit(solution)/shard_map/all_to_all | solution.py:94
Sparse Core Ops, SparseCore 0:
  126.9 72.1 all-gather.2
  201.8 68.8 all-gather.4
  319.5 114.7 all-reduce.2
where the time goes:
time: 446 us; the launch traced here: 445 us
  waiting for transfers between devices  237 us (53%)
  blocking collectives  110 us (25%)
  matrix products  46.3 us (10%)
  other arithmetic  19.1 us (4%)
  between operations  14 us (3%)
  starting transfers between devices  13.6 us (3%)
    psum x1, blocking collectives, shards(): low = lax.psum(partial_low.astype(jnp.bfloat16), 'gy')  74.6 us
    all_gather x1, waiting for transfers between devices, shards(): values = lax.all_gather(value_b, 'gx', axis=0, tiled=True)  71.5 us
    all_gather x1, waiting for transfers between devices, shards(): key_vectors = lax.all_gather(key_b, 'gx', axis=0, tiled=True)  71.4 us
    psum x1, waiting for transfers between devices, shards(): lax.psum(partial_out.astype(jnp.bfloat16), 'gy').astype(jnp.float32)  69.8 us
    psum x1, blocking collectives, shards(): lax.psum((jnp.sum(query * query, axis=(1, 2)), jnp.sum(key_raw * key_raw,...  35.5 us
    dot_general x16, matrix products, attend(): jnp.einsum('htk,khe->hte', weights.astype(jnp.bfloat16), values, preferre...  21.9 us
    dot_general x16, matrix products, attend(): jnp.einsum('the,khe->htk', query_b, key_vectors, preferred_element_type=j...  19 us
    all_to_all x1, waiting for transfers between devices, shards(): lax.all_to_all(pages[order], 'gx', split_axis=0, concat_axis=0, tiled=True)  13.7 us
  transfers between devices with their start and end apart: 5, of which 5 were waited for; matrix products, arithmetic and copies ran while one was open for 2% of the time, Pallas kernels for 0%

commit v1 on v0

--- a/solution.py
+++ b/solution.py
@@ -122,7 +122,9 @@
         jnp.zeros((heads_here, count, HEAD_SIZE), jnp.float32),
     )
     key_vectors = lax.all_gather(key_b, "gx", axis=0, tiled=True)
-    values = lax.all_gather(value_b, "gx", axis=0, tiled=True)
+    values = jnp.concatenate(
+        lax.all_to_all(jnp.stack([value_b] * lax.axis_size("gx")), "gx", 0, 0), axis=0
+    )
     size = key_vectors.shape[0]
     block = 512
 

time: 446 us -> 423 us (0.948)
  waiting for transfers between devices: 237 us -> 200 us
  starting transfers between devices: 13.6 us -> 25.9 us
    all_gather x1 -> x0, waiting for transfers between devices: 71.5 us -> none  [shards(): values = lax.all_gather(value_b, 'gx', axis=0, tiled=True)]
    all_gather x1, waiting for transfers between devices: 71.4 us -> 105 us  [shards(): key_vectors = lax.all_gather(key_b, 'gx', axis=0, tiled=True)]
    all_to_all x0 -> x1, starting transfers between devices: none -> 15.4 us  [shards(): lax.all_to_all(jnp.stack([value_b] * lax.axis_size('gx')), 'gx', 0, 0)]
    all_to_all x0 -> x1, waiting for transfers between devices: none -> 4.63 us  [shards(): lax.all_to_all(jnp.stack([value_b] * lax.axis_size('gx')), 'gx', 0, 0)]
where the time goes in v1:
time: 423 us; the launch traced here: 422 us
  waiting for transfers between devices  200 us (47%)
  blocking collectives  110 us (26%)
  matrix products  46.3 us (11%)
  starting transfers between devices  25.9 us (6%)
  other arithmetic  18.5 us (4%)
  between operations  14.3 us (3%)
  local copies, waits for them, and re-layouts  5.73 us (1%)
    all_gather x1, waiting for transfers between devices, shards(): key_vectors = lax.all_gather(key_b, 'gx', axis=0, tiled=True)  105 us
    psum x1, blocking collectives, shards(): low = lax.psum(partial_low.astype(jnp.bfloat16), 'gy')  74.6 us
    psum x1, waiting for transfers between devices, shards(): lax.psum(partial_out.astype(jnp.bfloat16), 'gy').astype(jnp.float32)  67.6 us
    psum x1, blocking collectives, shards(): lax.psum((jnp.sum(query * query, axis=(1, 2)), jnp.sum(key_raw * key_raw,...  35.5 us
    dot_general x16, matrix products, attend(): jnp.einsum('htk,khe->hte', weights.astype(jnp.bfloat16), values, preferre...  21.9 us
    dot_general x16, matrix products, attend(): jnp.einsum('the,khe->htk', query_b, key_vectors, preferred_element_type=j...  19 us
    all_to_all x1, starting transfers between devices, shards(): lax.all_to_all(jnp.stack([value_b] * lax.axis_size('gx')), 'gx', 0, 0)  15.4 us
    all_to_all x1, waiting for transfers between devices, shards(): lax.all_to_all(pages[order], 'gx', split_axis=0, concat_axis=0, tiled=True)  13.7 us
  transfers between devices with their start and end apart: 5, of which 5 were waited for; matrix products, arithmetic and copies ran while one was open for 2% of the time, Pallas kernels for 0%

profile of v1, /device:TPU:32, one launch (start us, length us, event | category | flops | bytes accessed | tf_op | source)
XLA Modules:
  0.0 422.2 jit_solution(15079948194238390208)
XLA Ops:
  10.4 1.7 fusion.33
  12.1 74.6 %psum.28 = bf16[256,3,16]{0,2,1:T(8,128)(2,1)S(1)} all-reduce(bf16[256,3,16]{0,2,1:T(8,128)(2,1)S(1)} %bitcast.117), channel_id=1, replica_groups=mesh['gx'=32,'gy'=16] {'gy'}, use_global_device_ids=true, to_apply=%region_4.5 | all-reduce | flops 12288 | bytes 49152 | tf_op jit(solution)/shard_map/psum | solution.py:64
  86.7 1.9 fusion.30
  89.2 35.5 %all-reduce = (f32[256]{0:T(256)S(1)}, f32[256]{0:T(256)S(1)}) all-reduce(f32[256]{0:T(256)S(1)} %get-tuple-element.231, f32[256]{0:T(256)S(1)} %get-tuple-element.230), channel_id=1, replica_groups=mesh['gx'=32,'gy'=16] {'gy'}, use_global_device_ids=true, to_apply=%region_6.7 | all-reduce | flops 512 | bytes 4096 | tf_op jit(solution)/shard_map/psum | solution.py:77
  124.8 1.8 stack.2
  126.6 15.4 %all-to-all-start = ((bf16[32,256,1,128]{3,1,2,0:T(8,128)(2,1)}), bf16[32,256,1,128]{3,1,2,0:T(8,128)(2,1)}, u32[]{:S(2)}, u32[]{:S(2)}) async-start(bf16[32,256,1,128]{3,1,2,0:T(8,128)(2,1)} %stack.2), calls=%async_computation | async-start | bytes 4194304 | tf_op jit(solution)/shard_map/all_to_all | solution.py:126
  143.7 104.6 %all-gather.2.cloned.1.call-done = bf16[8192,1,128]{2,0,1:T(8,128)(2,1)} async-done(((bf16[256,1,128]{2,0,1:T(8,128)(2,1)}), bf16[8192,1,128]{2,0,1:T(8,128)(2,1)}) %all-gather.2.cloned.1.call-update) | async-done | bytes 2097168 | tf_op jit(solution)/shard_map/all_gather | solution.py:124
  248.3 4.6 %all-to-all-done = bf16[32,256,1,128]{3,1,2,0:T(8,128)(2,1)} async-done(((bf16[32,256,1,128]{3,1,2,0:T(8,128)(2,1)}), bf16[32,256,1,128]{3,1,2,0:T(8,128)(2,1)}, u32[]{:S(2)}, u32[]{:S(2)}) %all-to-all-start) | async-done | bytes 2097184 | tf_op jit(solution)/shard_map/all_to_all | solution.py:126
  252.9 47.3 %while.18 = (s32[]{:T(128)}, f32[1,256]{1,0:T(1,128)S(1)}, f32[1,256]{1,0:T(1,128)S(1)}, f32[1,256,128]{2,1,0:T(8,128)S(1)}, s32[256]{0:T(256)S(1)}, /*index=5*/...) while((s32[]{:T(128)}, f32[1,256]{1,0:T(1,128)S(1)}, ...), condition=%wide.region_14.15_spmd.clone, body=%wide.region_10.14_spmd.clone.sunk | while | flops 69574144 | bytes 2204895 | solution.py:138
  254.5 1.4 fusion.75
  257.4 1.4 fusion.75
  260.4 1.4 fusion.75
  263.3 1.4 fusion.75
  266.3 1.4 fusion.75
  269.2 1.4 fusion.75
  272.2 1.4 fusion.75
  275.1 1.4 fusion.75
  278.1 1.4 fusion.75
  281.0 1.4 fusion.75
  284.0 1.4 fusion.75
  289.9 1.4 fusion.75
  295.8 1.4 fusion.75
  300.2 1.5 convolution_convert_fusion
  301.7 1.6 sort.31
  304.7 5.4 %all-to-all-start.2 = ((s32[32,1,1]{2,1,0:T(1,128)}), s32[32,1,1]{2,1,0:T(1,128)S(1)}, u32[]{:S(2)}, u32[]{:S(2)}) async-start(s32[32,1,1]{2,1,0:T(1,128)} %copy.30), calls=%async_computation.2 | async-start | bytes 32768 | tf_op jit(solution)/shard_map/all_to_all | solution.py:95
  311.4 9.8 %all-to-all-done.2 = s32[32,1,1]{2,1,0:T(1,128)S(1)} async-done(((s32[32,1,1]{2,1,0:T(1,128)}), s32[32,1,1]{2,1,0:T(1,128)S(1)}, u32[]{:S(2)}, u32[]{:S(2)}) %all-to-all-start.2) | async-done | bytes 160 | tf_op jit(solution)/shard_map/all_to_all | solution.py:95
  321.2 5.0 %all-to-all-start.1 = ((bf16[32,8,1,256]{3,1,2,0:T(8,128)(2,1)}), bf16[32,8,1,256]{3,1,2,0:T(8,128)(2,1)S(1)}, u32[]{:S(2)}, u32[]{:S(2)}) async-start(bf16[32,8,1,256]{3,1,2,0:T(8,128)(2,1)} %bitcast.28), calls=%async_computation.1 | async-start | bytes 262144 | tf_op jit(solution)/shard_map/all_to_all | solution.py:94
  326.9 1.7 sort.32
  328.6 13.7 %all-to-all-done.1 = bf16[32,8,1,256]{3,1,2,0:T(8,128)(2,1)S(1)} async-done(((bf16[32,8,1,256]{3,1,2,0:T(8,128)(2,1)}), bf16[32,8,1,256]{3,1,2,0:T(8,128)(2,1)S(1)}, u32[]{:S(2)}, u32[]{:S(2)}) %all-to-all-start.1) | async-done | bytes 131104 | tf_op jit(solution)/shard_map/all_to_all | solution.py:94
  343.6 67.6 %all-reduce.3.cloned.1.call-done = bf16[256,2048]{1,0:T(8,128)(2,1)} async-done(((bf16[256,2048]{1,0:T(8,128)(2,1)}), bf16[256,2048]{1,0:T(8,128)(2,1)}) %all-reduce.3.cloned.1.call-update) | async-done | bytes 1048592 | tf_op jit(solution)/shard_map/psum | solution.py:141
  411.1 1.5 fusion.24
  412.7 2.6 fusion.27
  (184 shorter events, 38.5 us)
Async XLA Ops:
  7.2 79.6 %copy-start = (bf16[2048,1,384]{2,0,1:T(8,128)(2,1)S(1)}, bf16[2048,1,384]{2,0,1:T(8,128)(2,1)}, u32[]{:S(2)}) copy-start(bf16[2048,1,384]{2,0,1:T(8,128)(2,1)} %param.19) | copy-start | bytes 4718596
  10.4 78.3 %copy-start.7 = (bf16[16,3,16,1,128]{4,2,3,1,0:T(8,128)(2,1)S(1)}, bf16[16,3,16,1,128]{4,2,3,1,0:T(8,128)(2,1)}, u32[]{:S(2)}) copy-start(bf16[16,3,16,1,128]{4,2,3,1,0:T(8,128)(2,1)} %param.21) | copy-start | bytes 589828
  88.7 36.0 %copy-start.5 = (f32[1,128]{1,0:T(1,128)S(1)}, f32[1,128]{1,0:T(1,128)}, u32[]{:S(2)}) copy-start(f32[1,128]{1,0:T(1,128)} %param.23) | copy-start | bytes 1540
  88.7 36.0 %copy-start.6 = (f32[1,128]{1,0:T(1,128)S(1)}, f32[1,128]{1,0:T(1,128)}, u32[]{:S(2)}) copy-start(f32[1,128]{1,0:T(1,128)} %param.22) | copy-start | bytes 1540
  126.6 126.2 %all-to-all-start = ((bf16[32,256,1,128]{3,1,2,0:T(8,128)(2,1)}), bf16[32,256,1,128]{3,1,2,0:T(8,128)(2,1)}, u32[]{:S(2)}, u32[]{:S(2)}) async-start(bf16[32,256,1,128]{3,1,2,0:T(8,128)(2,1)} %stack.2), calls=%async_computation | async-start | bytes 4194304 | tf_op jit(solution)/shard_map/all_to_all | solution.py:126
  142.1 106.2 %all-gather.2.cloned.1.call-start = ((), (), s32[]{:S(2)}) async-start(), calls=%async_computation.3 | async-start | bytes 2162688 | tf_op jit(solution)/shard_map/all_gather | solution.py:124
  143.5 267.6 %all-reduce.3.cloned.1.call-start = ((), (), s32[]{:S(2)}) async-start(), calls=%async_computation.4 | async-start | bytes 2097152 | tf_op jit(solution)/shard_map/psum | solution.py:141
  252.9 47.3 %copy-start.3 = (bf16[1,128,2048]{2,1,0:T(8,128)(2,1)S(1)}, bf16[1,128,2048]{2,1,0:T(8,128)(2,1)}, u32[]{:S(2)}) copy-start(bf16[1,128,2048]{2,1,0:T(8,128)(2,1)} %param.24) | copy-start | bytes 1572868
  300.1 1.5 copy-start.1
  301.6 111.0 %copy-start.2 = (bf16[256,2048]{1,0:T(8,128)(2,1)S(1)}, bf16[256,2048]{1,0:T(8,128)(2,1)}, u32[]{:S(2)}) copy-start(bf16[256,2048]{1,0:T(8,128)(2,1)} %param.14) | copy-start | bytes 3145732
  301.6 111.0 %copy-start.4 = (f32[2048]{0:T(1024)S(1)}, f32[2048]{0:T(1024)}, u32[]{:S(2)}) copy-start(f32[2048]{0:T(1024)} %param.25) | copy-start | bytes 24580
  304.7 16.6 %all-to-all-start.2 = ((s32[32,1,1]{2,1,0:T(1,128)}), s32[32,1,1]{2,1,0:T(1,128)S(1)}, u32[]{:S(2)}, u32[]{:S(2)}) async-start(s32[32,1,1]{2,1,0:T(1,128)} %copy.30), calls=%async_computation.2 | async-start | bytes 32768 | tf_op jit(solution)/shard_map/all_to_all | solution.py:95
  321.2 21.1 %all-to-all-start.1 = ((bf16[32,8,1,256]{3,1,2,0:T(8,128)(2,1)}), bf16[32,8,1,256]{3,1,2,0:T(8,128)(2,1)S(1)}, u32[]{:S(2)}, u32[]{:S(2)}) async-start(bf16[32,8,1,256]{3,1,2,0:T(8,128)(2,1)} %bitcast.28), calls=%async_computation.1 | async-start | bytes 262144 | tf_op jit(solution)/shard_map/all_to_all | solution.py:94
Sparse Core Ops, SparseCore 0:
  145.6 102.6 all-gather.1
  301.8 109.3 all-reduce.2
